TPU v7x, 256 devices: a whole 4x4x8 slice. The times are simulated.
256 devices in a mesh: gz: 8 (over x, core), gx: 32 (over z, y).
Axes of the slice: x: 4, y: 4, z: 8, core: 2. Of those that a mesh axis runs over, the one named last changes fastest.
Arguments:
- volume: float32 [256, 512, 256], P('gz', 'gx')
- measured: float32 [2, 256, 2048], P(None, 'gz')
- weight_blocks: bfloat16 [64, 128, 128], replicated, may hold values from 0 to 2
- view_order: int32 [2], replicated, may hold values from 0 to 1, each once
- tile_voxel: int32 [2, 8, 16384], P(None, 'gz', 'gx'), may hold values from 0 to 1023
- tile_column: int32 [2, 8, 16384], P(None, 'gz', 'gx'), may hold values from 0 to 15
- tile_block: int32 [2, 8, 16384], P(None, 'gz', 'gx'), may hold values from 0 to 63
- entry_count: int32 [2, 8, 32], P(None, 'gz', 'gx'), may hold values from 1 to 512, as said below
Outputs:
- volume_out: float32 [256, 512, 256], P('gz', 'gx')
Inputs may be any that keep to these rules, and one draw needn't show every extreme that they name: Entries of block (a, c) of view v at or past entry_count[v, a, c] are not used; in every view some block has 512 live entries.
All inputs are finite; a program needn't handle non-finite values.
Results may differ from a plain program's by a relative error of at most 0.0027.
Values may be sent and summed in bfloat16 or wider, within the bound.
A program may use at most 64 MiB of HBM per device.

v0:
```python
import jax
import jax.numpy as jnp
from jax import lax
from jax.sharding import PartitionSpec as P

TV_STEPS = 4
smooth_floor = 0.01
step_gain = 0.25
norm_floor = 1e-06
group_rows = 128


def padded_2(cells, sides, width):
    for axis, dim in sides:
        count = lax.axis_size(axis)
        ends = count - 1
        head = lax.slice_in_dim(cells, 0, width, axis=dim)
        tail = lax.slice_in_dim(cells, cells.shape[dim] - width, cells.shape[dim], axis=dim)
        cells = jnp.concatenate(
            [
                lax.ppermute(tail, axis, [(i, (i + 1) % count) for i in range(ends)]),
                cells,
                lax.ppermute(head, axis, [((i + 1) % count, i) for i in range(ends)]),
            ],
            axis=dim,
        )
    return cells


def tv_grad(padded):
    base_cells = padded[:-1, :-1, :-1]
    diff_z = padded[1:, :-1, :-1] - base_cells
    diff_x = padded[:-1, 1:, :-1] - base_cells
    diff_y = padded[:-1, :-1, 1:] - base_cells
    inverse = lax.rsqrt(diff_z * diff_z + diff_x * diff_x + diff_y * diff_y + smooth_floor)
    flow_z = diff_z * inverse
    flow_x = diff_x * inverse
    flow_y = diff_y * inverse
    flow_all = flow_z + flow_x + flow_y
    return flow_z[:-1, 1:, 1:] + flow_x[1:, :-1, 1:] + flow_y[1:, 1:, :-1] - flow_all[1:, 1:, 1:]


def pad_depth(field):
    return jnp.pad(field, ((0, 0), (0, 0), (1, 1)))


def body(
    volume, measured, weight_blocks, view_order, tile_voxel, tile_column, tile_block, entry_count
):
    depth_z, depth_x, depth_y = volume.shape
    tiles_y = depth_y // group_rows
    tiles_u = measured.shape[2] // group_rows
    slab_tiles = depth_z * tiles_u
    plane_tiles = depth_x * tiles_y
    row_weight = jnp.sum(weight_blocks, axis=2, dtype=jnp.float32)
    col_weight = jnp.sum(weight_blocks, axis=1, dtype=jnp.float32)
    offsets = jnp.arange(group_rows, dtype=jnp.int32)
    current = volume
    for turn_index in range(view_order.shape[0]):
        view_index = view_order[turn_index]
        voxel_list = lax.dynamic_index_in_dim(tile_voxel, view_index, 0, keepdims=False)[0]
        column_list = lax.dynamic_index_in_dim(tile_column, view_index, 0, keepdims=False)[0]
        block_list = lax.dynamic_index_in_dim(tile_block, view_index, 0, keepdims=False)[0]
        live_count = lax.dynamic_index_in_dim(entry_count, view_index, 0, keepdims=False)[0, 0]
        rounds = (live_count + group_rows - 1) // group_rows
        voxel_tiles = current.astype(jnp.bfloat16).reshape(-1, group_rows)

        def gather_group(index):
            begin = index * group_rows
            voxels = lax.dynamic_slice_in_dim(voxel_list, begin, group_rows)
            columns = lax.dynamic_slice_in_dim(column_list, begin, group_rows)
            chosen = lax.dynamic_slice_in_dim(block_list, begin, group_rows)
            weight = (begin + offsets < live_count).astype(jnp.float32)[:, None]
            detector = voxels // plane_tiles * tiles_u + columns
            return (voxels, detector, chosen, weight)

        def forward(index, carry):
            projection, ray_sum = carry
            voxels, detector, chosen, weight = gather_group(index)
            product = jnp.einsum(
                "ejk,ek->ej",
                weight_blocks[chosen],
                voxel_tiles[voxels],
                preferred_element_type=jnp.float32,
            )
            return (
                projection.at[detector].add(product * weight),
                ray_sum.at[detector].add(row_weight[chosen] * weight),
            )

        empty = jnp.zeros((slab_tiles, group_rows), jnp.float32)
        projection, ray_sum = lax.fori_loop(0, rounds, forward, (empty, empty))
        target = lax.dynamic_index_in_dim(measured, view_index, 0, keepdims=False).reshape(
            slab_tiles, group_rows
        )
        projection, ray_sum = (
            lax.psum(projection.astype(jnp.bfloat16), "gx").astype(jnp.float32),
            lax.psum(ray_sum.astype(jnp.bfloat16), "gx").astype(jnp.float32),
        )
        residual = ((target - projection) / (ray_sum + 1.0)).astype(jnp.bfloat16)

        def backward(index, carry):
            change, voxel_sum = carry
            voxels, detector, chosen, weight = gather_group(index)
            product = jnp.einsum(
                "ejk,ej->ek",
                weight_blocks[chosen],
                residual[detector],
                preferred_element_type=jnp.float32,
            )
            return (
                change.at[voxels].add(product * weight),
                voxel_sum.at[voxels].add(col_weight[chosen] * weight),
            )

        blank = jnp.zeros((voxel_tiles.shape[0], group_rows), jnp.float32)
        change, voxel_sum = lax.fori_loop(0, rounds, backward, (blank, blank))
        current = current + (change / (voxel_sum + 1.0)).reshape(current.shape)
    art_volume = jnp.maximum(current, 0.0)
    difference = art_volume - volume
    change_part = jnp.sum(difference * difference)
    change_total = None
    change_total = lax.psum(change_part, ("gz", "gx"))
    smooth = art_volume
    for sweep_index in range(TV_STEPS):
        padded = padded_2(smooth, (("gz", 0), ("gx", 1)), 1)
        slope = tv_grad(pad_depth(padded))
        slope_part = jnp.sum(slope * slope)
        if sweep_index == 0:
            slope_total = lax.psum(slope_part, ("gz", "gx"))
        else:
            slope_total = lax.psum(slope_part, ("gz", "gx"))
        change_total, scale_now = (
            change_total,
            step_gain * jnp.sqrt(change_total) / jnp.sqrt(slope_total + norm_floor),
        )
        smooth = smooth - scale_now * slope
    return smooth


def solution(mesh):
    return jax.shard_map(
        body,
        mesh=mesh,
        in_specs=(
            P("gz", "gx", None),
            P(None, "gz", None),
            P(),
            P(),
            P(None, "gz", "gx"),
            P(None, "gz", "gx"),
            P(None, "gz", "gx"),
            P(None, "gz", "gx"),
        ),
        out_specs=P("gz", "gx", None),
        check_vma=False,
    )
```

profile of v0, /device:TPU:1, one launch (start us, length us, event | category | flops | bytes accessed | tf_op | source)
XLA Modules:
  0.0 943.3 jit_solution(2549535672975663778)
XLA Ops:
  17.6 13.5 %while.60 = (s32[]{:T(128)}, f32[512,128]{1,0:T(8,128)S(1)}, f32[512,128]{1,0:T(8,128)}, s32[]{:T(128)}, s32[512]{0:T(512)S(1)}, /*index=5*/s32[512]{0:T(512)S(1...) while((s32[]{:T(128)}, f32[512,128]{1,0:T(8,128)S(1)}, ...), condition=%wide.region_4.5_spmd.clone, body=%wide.region_1.4_spmd.clone.sunk | while | flops 4265478 | bytes 13388487 | solution.py:92
  21.5 4.4 fusion.99
  36.0 180.4 %all-reduce.12.cloned.1.call-done = (bf16[512,128]{1,0:T(8,128)(2,1)}, bf16[512,128]{1,0:T(8,128)(2,1)}) async-done(((bf16[512,128]{1,0:T(8,128)(2,1)}, bf16[512,128]{1,0:T(8,128)(2,1)}), (bf16[512,128]{1,0:T(8,128)(2,1)}, bf16[512,128]{1,0:T(8,128)(2,1)})) %all-reduce.12.cloned.1.call-update) | async-done | bytes 262160 | tf_op jit(solution)/shard_map/psum | solution.py:98
  219.1 14.2 %while.61 = (s32[]{:T(128)}, f32[1024,128]{1,0:T(8,128)}, f32[1024,128]{1,0:T(8,128)}, s32[]{:T(128)}, s32[512]{0:T(512)S(1)}, /*index=5*/s32[512]{0:T(512)S(1)}...) while((s32[]{:T(128)}, f32[1024,128]{1,0:T(8,128)}, ...), condition=%wide.region_11.12_spmd.clone, body=%wide.region_8.11_spmd.clone.sunk | while | flops 4265478 | bytes 13912775 | solution.py:117
  223.0 3.4 fusion.104
  230.1 3.3 scatter_custom_fusion.47
  241.9 14.9 %while.62 = (s32[]{:T(128)}, f32[512,128]{1,0:T(8,128)}, f32[512,128]{1,0:T(8,128)}, s32[]{:T(128)}, s32[512]{0:T(512)S(1)}, /*index=5*/s32[512]{0:T(512)S(1)}, ...) while((s32[]{:T(128)}, f32[512,128]{1,0:T(8,128)}, ...), condition=%wide.region_15.16_spmd.clone, body=%wide.region_12.15_spmd.clone.sunk | while | flops 4265478 | bytes 13388487 | solution.py:92
  245.7 4.4 fusion.109
  260.8 227.2 %all-reduce.10.cloned.1.call-done = (bf16[512,128]{1,0:T(8,128)(2,1)}, bf16[512,128]{1,0:T(8,128)(2,1)}) async-done(((bf16[512,128]{1,0:T(8,128)(2,1)}, bf16[512,128]{1,0:T(8,128)(2,1)}), (bf16[512,128]{1,0:T(8,128)(2,1)}, bf16[512,128]{1,0:T(8,128)(2,1)})) %all-reduce.10.cloned.1.call-update) | async-done | bytes 262160 | tf_op jit(solution)/shard_map/psum | solution.py:98
  490.0 12.7 %while.63 = (s32[]{:T(128)}, f32[1024,128]{1,0:T(8,128)S(1)}, f32[1024,128]{1,0:T(8,128)}, s32[]{:T(128)}, s32[512]{0:T(512)S(1)}, /*index=5*/s32[512]{0:T(512)S...) while((s32[]{:T(128)}, f32[1024,128]{1,0:T(8,128)S(1)}, ...), condition=%wide.region_21.22_spmd.clone, body=%wide.region_18.21_spmd.clone.sunk | while | flops 4265478 | bytes 13912775 | solution.py:117
  493.8 3.4 fusion.114
  499.4 3.3 scatter_custom_fusion.55
  504.9 8.1 collective-permute-start
  521.3 3.4 collective-permute-done.3
  527.9 113.9 %all-reduce.4 = (f32[]{:T(128)}, f32[]{:T(128)}) all-reduce(f32[]{:T(128)} %get-tuple-element.839, f32[]{:T(128)} %get-tuple-element.837), channel_id=1, replica_groups=mesh['gz'=8,'gx'=32] {'gz','gx'}, use_global_device_ids=true, to_apply=%region_23.24 | all-reduce | flops 2 | bytes 16 | tf_op jit(solution)/shard_map/psum | solution.py:123
  643.4 3.5 collective-permute-start.4
  654.8 3.6 collective-permute-done.7
  661.7 77.6 %psum.69 = f32[]{:T(128)} all-reduce(f32[]{:T(128)} %get-tuple-element.833), channel_id=1, replica_groups=mesh['gz'=8,'gx'=32] {'gz','gx'}, use_global_device_ids=true, to_apply=%region_27.28 | all-reduce | flops 1 | bytes 8 | tf_op jit(solution)/shard_map/psum | solution.py:132
  740.1 3.5 collective-permute-start.8
  751.6 3.4 collective-permute-done.11
  758.3 78.8 %psum.70 = f32[]{:T(128)} all-reduce(f32[]{:T(128)} %get-tuple-element.829), channel_id=1, replica_groups=mesh['gz'=8,'gx'=32] {'gz','gx'}, use_global_device_ids=true, to_apply=%region_29.30 | all-reduce | flops 1 | bytes 8 | tf_op jit(solution)/shard_map/psum | solution.py:132
  837.8 3.5 collective-permute-start.12
  849.2 3.6 collective-permute-done.15
  856.0 78.8 %psum.71 = f32[]{:T(128)} all-reduce(f32[]{:T(128)} %get-tuple-element.825), channel_id=1, replica_groups=mesh['gz'=8,'gx'=32] {'gz','gx'}, use_global_device_ids=true, to_apply=%region_31.32 | all-reduce | flops 1 | bytes 8 | tf_op jit(solution)/shard_map/psum | solution.py:132
  (127 shorter events, 109.4 us)
Async XLA Ops:
  6.5 10.1 %copy-start.1 = (f32[32,16,256]{2,1,0:T(8,128)S(1)}, f32[32,16,256]{2,1,0:T(8,128)}, u32[]{:S(2)}) copy-start(f32[32,16,256]{2,1,0:T(8,128)} %param.16) | copy-start | bytes 1572868
  6.5 209.8 %all-reduce.12.cloned.1.call-start = ((), (), s32[]{:S(2)}) async-start(), calls=%async_computation.1 | async-start | bytes 524288 | tf_op jit(solution)/shard_map/psum | solution.py:98
  14.3 2.6 copy-start.3
  14.3 2.6 copy-start.4
  14.3 3.4 copy-start
  33.4 454.6 %all-reduce.10.cloned.1.call-start = ((), (), s32[]{:S(2)}) async-start(), calls=%async_computation | async-start | bytes 524288 | tf_op jit(solution)/shard_map/psum | solution.py:98
  502.7 1.3 copy-start.2
  504.9 10.0 %collective-permute-start = (f32[1,16,256]{2,1,0:T(8,128)S(1)}, f32[1,16,256]{2,1,0:T(8,128)S(1)}, u32[]{:S(2)}, u32[]{:S(2)}) collective-permute-start(f32[1,16,256]{2,1,0:T(8,128)S(1)} %get-tuple-element.879), channel_id=1, source_target_pairs={{0,32},{32,64},{64,96},{96,128},{128,160},{160,192},{192,224},{1,3... | collective-permute-start | bytes 49160 | tf_op jit(solution)/shard_map/ppermute | solution.py:21
  513.0 5.1 collective-permute-start.1
  518.1 3.3 collective-permute-start.2
  520.0 4.7 collective-permute-start.3
  643.4 5.5 collective-permute-start.4
  647.0 5.1 collective-permute-start.5
  652.1 2.7 collective-permute-start.6
  653.5 4.9 collective-permute-start.7
  740.1 5.4 collective-permute-start.8
  743.6 5.1 collective-permute-start.9
  748.7 2.9 collective-permute-start.10
  750.1 4.9 collective-permute-start.11
  837.8 5.4 collective-permute-start.12
  841.3 5.1 collective-permute-start.13
  846.5 2.7 collective-permute-start.14
  847.9 4.9 collective-permute-start.15
Sparse Core Ops, SparseCore 0:
  33.6 182.7 all-reduce.11
  260.1 227.8 all-reduce.9
where the time goes:
time: 946 us; the launch traced here: 943 us
  waiting for transfers between devices  434 us (46%)
  blocking collectives  349 us (37%)
  other arithmetic  55.2 us (6%)
  starting transfers between devices  37.9 us (4%)
  local copies, waits for them, and re-layouts  28.9 us (3%)
  between operations  22.3 us (2%)
  matrix products  15.6 us (2%)
    psum x2, waiting for transfers between devices, body(): lax.psum(ray_sum.astype(jnp.bfloat16), 'gx').astype(jnp.float32)  408 us
    psum x3, blocking collectives, body(): slope_total = lax.psum(slope_part, ('gz', 'gx'))  235 us
    psum x1, blocking collectives, body(): change_total = lax.psum(change_part, ('gz', 'gx'))  114 us
    ppermute x8, waiting for transfers between devices, padded_2(): lax.ppermute(head, axis, [((i + 1) % count, i) for i in range(ends)])  26.5 us
    ppermute x8, starting transfers between devices, padded_2(): lax.ppermute(tail, axis, [(i, (i + 1) % count) for i in range(ends)])  24.8 us
  transfers between devices with their start and end apart: 18, of which 10 were waited for; matrix products, arithmetic and copies ran while one was open for 0% of the time, Pallas kernels for 0%

commit v1 on v0

--- a/solution.py
+++ b/solution.py
@@ -129,7 +129,7 @@
         if sweep_index == 0:
             slope_total = lax.psum(slope_part, ("gz", "gx"))
         else:
-            slope_total = lax.psum(slope_part, ("gz", "gx"))
+            slope_total = lax.psum(lax.psum(slope_part, "gz"), "gx")
         change_total, scale_now = (
             change_total,
             step_gain * jnp.sqrt(change_total) / jnp.sqrt(slope_total + norm_floor),

time: 946 us -> 975 us (1.031)
  the two profiles are of different devices: /device:TPU:1 before, /device:TPU:128 now
where the time goes in v1:
time: 975 us; the launch traced here: 973 us
  waiting for transfers between devices  380 us (39%)
  blocking collectives  368 us (38%)
  other arithmetic  79.5 us (8%)
  starting transfers between devices  47.7 us (5%)
  local copies, waits for them, and re-layouts  43.7 us (4%)
  matrix products  31.2 us (3%)
  between operations  22.5 us (2%)
    psum x2, waiting for transfers between devices, body(): lax.psum(ray_sum.astype(jnp.bfloat16), 'gx').astype(jnp.float32)  364 us
    psum x6, blocking collectives, body(): slope_total = lax.psum(lax.psum(slope_part, 'gz'), 'gx')  269 us
    psum x1, blocking collectives, body(): change_total = lax.psum(change_part, ('gz', 'gx'))  99 us
    ppermute x8, starting transfers between devices, padded_2(): lax.ppermute(head, axis, [((i + 1) % count, i) for i in range(ends)])  33.9 us
  transfers between devices with their start and end apart: 18, of which 10 were waited for; matrix products, arithmetic and copies ran while one was open for 0% of the time, Pallas kernels for 0%

profile of v1, /device:TPU:128, one launch (start us, length us, event | category | flops | bytes accessed | tf_op | source)
XLA Modules:
  0.0 972.5 jit_solution(3804444494537859354)
XLA Ops:
  18.0 27.0 %while.60 = (s32[]{:T(128)}, f32[512,128]{1,0:T(8,128)S(1)}, f32[512,128]{1,0:T(8,128)}, s32[]{:T(128)}, s32[512]{0:T(512)S(1)}, /*index=5*/s32[512]{0:T(512)S(1...) while((s32[]{:T(128)}, f32[512,128]{1,0:T(8,128)S(1)}, ...), condition=%wide.region_4.5_spmd.clone, body=%wide.region_1.4_spmd.clone.sunk | while | flops 4265478 | bytes 13388487 | solution.py:92
  21.8 4.4 fusion.99
  35.3 4.4 fusion.99
  49.7 166.2 %all-reduce.12.cloned.1.call-done = (bf16[512,128]{1,0:T(8,128)(2,1)}, bf16[512,128]{1,0:T(8,128)(2,1)}) async-done(((bf16[512,128]{1,0:T(8,128)(2,1)}, bf16[512,128]{1,0:T(8,128)(2,1)}), (bf16[512,128]{1,0:T(8,128)(2,1)}, bf16[512,128]{1,0:T(8,128)(2,1)})) %all-reduce.12.cloned.1.call-update) | async-done | bytes 262160 | tf_op jit(solution)/shard_map/psum | solution.py:98
  218.7 28.4 %while.61 = (s32[]{:T(128)}, f32[1024,128]{1,0:T(8,128)}, f32[1024,128]{1,0:T(8,128)}, s32[]{:T(128)}, s32[512]{0:T(512)S(1)}, /*index=5*/s32[512]{0:T(512)S(1)}...) while((s32[]{:T(128)}, f32[1024,128]{1,0:T(8,128)}, ...), condition=%wide.region_11.12_spmd.clone, body=%wide.region_8.11_spmd.clone.sunk | while | flops 4265478 | bytes 13912775 | solution.py:117
  222.6 3.4 fusion.104
  255.7 29.5 %while.62 = (s32[]{:T(128)}, f32[512,128]{1,0:T(8,128)}, f32[512,128]{1,0:T(8,128)}, s32[]{:T(128)}, s32[512]{0:T(512)S(1)}, /*index=5*/s32[512]{0:T(512)S(1)}, ...) while((s32[]{:T(128)}, f32[512,128]{1,0:T(8,128)}, ...), condition=%wide.region_15.16_spmd.clone, body=%wide.region_12.15_spmd.clone.sunk | while | flops 4265478 | bytes 13388487 | solution.py:92
  259.5 4.4 fusion.109
  274.2 4.4 fusion.109
  289.2 197.8 %all-reduce.10.cloned.1.call-done = (bf16[512,128]{1,0:T(8,128)(2,1)}, bf16[512,128]{1,0:T(8,128)(2,1)}) async-done(((bf16[512,128]{1,0:T(8,128)(2,1)}, bf16[512,128]{1,0:T(8,128)(2,1)}), (bf16[512,128]{1,0:T(8,128)(2,1)}, bf16[512,128]{1,0:T(8,128)(2,1)})) %all-reduce.10.cloned.1.call-update) | async-done | bytes 262160 | tf_op jit(solution)/shard_map/psum | solution.py:98
  489.0 25.1 %while.63 = (s32[]{:T(128)}, f32[1024,128]{1,0:T(8,128)S(1)}, f32[1024,128]{1,0:T(8,128)}, s32[]{:T(128)}, s32[512]{0:T(512)S(1)}, /*index=5*/s32[512]{0:T(512)S...) while((s32[]{:T(128)}, f32[1024,128]{1,0:T(8,128)S(1)}, ...), condition=%wide.region_21.22_spmd.clone, body=%wide.region_18.21_spmd.clone.sunk | while | flops 4265478 | bytes 13912775 | solution.py:117
  492.8 3.4 fusion.114
  518.9 3.5 collective-permute-done.1
  524.5 7.0 collective-permute-start.3
  536.5 99.0 %all-reduce.4 = (f32[]{:T(128)}, f32[]{:T(128)}) all-reduce(f32[]{:T(128)} %get-tuple-element.839, f32[]{:T(128)} %get-tuple-element.837), channel_id=1, replica_groups=mesh['gz'=8,'gx'=32] {'gz','gx'}, use_global_device_ids=true, to_apply=%region_23.24 | all-reduce | flops 2 | bytes 16 | tf_op jit(solution)/shard_map/psum | solution.py:123
  645.0 7.1 collective-permute-start.7
  656.9 14.4 %psum.90 = f32[]{:T(128)} all-reduce(f32[]{:T(128)} %get-tuple-element.833), channel_id=1, replica_groups=mesh['gz'=8,'gx'=32] {'gz'}, use_global_device_ids=true, to_apply=%region_27.28 | all-reduce | flops 1 | bytes 8 | tf_op jit(solution)/shard_map/psum | solution.py:132
  671.3 75.6 %psum.91 = f32[]{:T(128)} all-reduce(f32[]{:T(128)} %psum.90), channel_id=1, replica_groups=mesh['gz'=8,'gx'=32] {'gx'}, use_global_device_ids=true, to_apply=%region_28.29 | all-reduce | flops 1 | bytes 8 | tf_op jit(solution)/shard_map/psum | solution.py:132
  754.0 7.5 collective-permute-start.11
  766.1 13.8 %psum.92 = f32[]{:T(128)} all-reduce(f32[]{:T(128)} %get-tuple-element.829), channel_id=1, replica_groups=mesh['gz'=8,'gx'=32] {'gz'}, use_global_device_ids=true, to_apply=%region_30.31 | all-reduce | flops 1 | bytes 8 | tf_op jit(solution)/shard_map/psum | solution.py:132
  779.9 75.6 %psum.93 = f32[]{:T(128)} all-reduce(f32[]{:T(128)} %psum.92), channel_id=1, replica_groups=mesh['gz'=8,'gx'=32] {'gx'}, use_global_device_ids=true, to_apply=%region_31.32 | all-reduce | flops 1 | bytes 8 | tf_op jit(solution)/shard_map/psum | solution.py:132
  862.6 7.2 collective-permute-start.15
  874.7 13.8 %psum.94 = f32[]{:T(128)} all-reduce(f32[]{:T(128)} %get-tuple-element.825), channel_id=1, replica_groups=mesh['gz'=8,'gx'=32] {'gz'}, use_global_device_ids=true, to_apply=%region_33.34 | all-reduce | flops 1 | bytes 8 | tf_op jit(solution)/shard_map/psum | solution.py:132
  888.5 75.6 %psum.95 = f32[]{:T(128)} all-reduce(f32[]{:T(128)} %psum.94), channel_id=1, replica_groups=mesh['gz'=8,'gx'=32] {'gx'}, use_global_device_ids=true, to_apply=%region_34.35 | all-reduce | flops 1 | bytes 8 | tf_op jit(solution)/shard_map/psum | solution.py:132
  (166 shorter events, 161.5 us)
Async XLA Ops:
  6.5 10.5 %copy-start.1 = (f32[32,16,256]{2,1,0:T(8,128)S(1)}, f32[32,16,256]{2,1,0:T(8,128)}, u32[]{:S(2)}) copy-start(f32[32,16,256]{2,1,0:T(8,128)} %param.16) | copy-start | bytes 1572868
  6.5 209.4 %all-reduce.12.cloned.1.call-start = ((), (), s32[]{:S(2)}) async-start(), calls=%async_computation.1 | async-start | bytes 524288 | tf_op jit(solution)/shard_map/psum | solution.py:98
  14.7 2.6 copy-start.3
  14.7 2.6 copy-start.4
  14.7 3.4 copy-start
  47.3 439.7 %all-reduce.10.cloned.1.call-start = ((), (), s32[]{:S(2)}) async-start(), calls=%async_computation | async-start | bytes 524288 | tf_op jit(solution)/shard_map/psum | solution.py:98
  514.1 1.3 copy-start.2
  516.3 2.6 collective-permute-start
  517.5 4.8 collective-permute-start.1
  522.4 9.2 collective-permute-start.2
  524.5 8.6 collective-permute-start.3
  636.9 3.1 collective-permute-start.4
  638.6 4.2 collective-permute-start.5
  642.9 9.2 collective-permute-start.6
  645.0 8.7 collective-permute-start.7
  747.6 2.6 collective-permute-start.8
  748.9 3.1 collective-permute-start.9
  752.1 9.4 collective-permute-start.10
  754.0 8.8 collective-permute-start.11
  856.3 2.6 collective-permute-start.12
  857.6 3.1 collective-permute-start.13
  860.7 9.2 collective-permute-start.14
  862.6 8.8 collective-permute-start.15
Sparse Core Ops, SparseCore 0:
  47.4 168.5 all-reduce.11
  288.6 198.3 all-reduce.9
